TPU v7x, 32 devices: a whole 2x2x4 slice. The times are simulated.
32 devices in a mesh: dp: 16 (over z, x, core), seq: 2 (over y).
Axes of the slice: x: 2, y: 2, z: 4, core: 2. Of those that a mesh axis runs over, the one named last changes fastest.
Arguments:
- tokens: float32 [32, 1024, 768], P('dp', 'seq'), may hold values from -6 to 6
- segments: int32 [32, 1024], P('dp'), may hold values from 0 to 3, never falling along the last dimension, each value on 1 to 512 neighbouring positions
- padding: int32 [32, 1024], P('dp'), may hold values 0 or 1
- query_weight: bfloat16 [768, 768], P(('dp', 'seq')), may hold values from -0.3125 to 0.3125
- query_bias: bfloat16 [768], P(('dp', 'seq')), may hold values from -1.25 to 1.25
- key_weight: bfloat16 [768, 768], P(('dp', 'seq')), may hold values from -0.3125 to 0.3125
- value_weight: bfloat16 [768, 768], P(('dp', 'seq')), may hold values from -0.21875 to 0.21875
- value_bias: bfloat16 [768], P(('dp', 'seq')), may hold values from -1.25 to 1.25
- output_weight: bfloat16 [768, 768], P(('dp', 'seq')), may hold values from -0.875 to 0.875
- output_bias: bfloat16 [768], P(('dp', 'seq')), may hold values from -1.25 to 1.25
- first_gain: bfloat16 [768], P(('dp', 'seq')), may hold values from 0.5 to 1.5
- first_shift: bfloat16 [768], P(('dp', 'seq')), may hold values from -1.25 to 1.25
- inner_weight: bfloat16 [768, 3072], P(('dp', 'seq')), may hold values from -0.21875 to 0.21875
- inner_bias: bfloat16 [3072], P(('dp', 'seq')), may hold values from -1.25 to 1.25
- outer_weight: bfloat16 [3072, 768], P(('dp', 'seq')), may hold values from -0.109375 to 0.109375
- outer_bias: bfloat16 [768], P(('dp', 'seq')), may hold values from -1.25 to 1.25
- second_gain: bfloat16 [768], P(('dp', 'seq')), may hold values from 0.5 to 1.5
- second_shift: bfloat16 [768], P(('dp', 'seq')), may hold values from -1.25 to 1.25
- cotangent: float32 [32, 1024, 768], P('dp', 'seq'), may hold values from -6 to 6
Outputs:
- layer_output: float32 [32, 1024, 768], P('dp', 'seq')
- input_grad: float32 [32, 1024, 768], P('dp', 'seq')
- query_weight_grad: float32 [768, 768], P(('dp', 'seq'))
- query_bias_grad: float32 [768], P(('dp', 'seq'))
- key_weight_grad: float32 [768, 768], P(('dp', 'seq'))
- value_weight_grad: float32 [768, 768], P(('dp', 'seq'))
- value_bias_grad: float32 [768], P(('dp', 'seq'))
- output_weight_grad: float32 [768, 768], P(('dp', 'seq'))
- output_bias_grad: float32 [768], P(('dp', 'seq'))
- first_gain_grad: float32 [768], P(('dp', 'seq'))
- first_shift_grad: float32 [768], P(('dp', 'seq'))
- inner_weight_grad: float32 [768, 3072], P(('dp', 'seq'))
- inner_bias_grad: float32 [3072], P(('dp', 'seq'))
- outer_weight_grad: float32 [3072, 768], P(('dp', 'seq'))
- outer_bias_grad: float32 [768], P(('dp', 'seq'))
- second_gain_grad: float32 [768], P(('dp', 'seq'))
- second_shift_grad: float32 [768], P(('dp', 'seq'))
Inputs may be any that keep to these rules, and one draw needn't show every extreme that they name: `segments`: in each sequence the segment numbers never fall; each document is a run of 1 to 512 tokens, and one has exactly 512.
All inputs are finite; a program needn't handle non-finite values. No bound on the sum of `padding` on one device may be relied on, other than what follows from the above.
Results may differ from a plain program's by a relative error of at most 0.014.
The roundings to bfloat16 on the way count: a program that leaves them out, or rounds other values in their place, can miss the bound.
Values may be sent and summed in bfloat16 or wider, within the bound.
A program may use at most 192 MiB of HBM per device.

v0:
```python
import jax
import jax.numpy as jnp
from jax import lax
from jax.sharding import PartitionSpec as P

HEADS = 12
HEAD_DIM = 64


neg_big = -1e30


def matmul(left, right):
    return jnp.dot(left, right, preferred_element_type=jnp.float32)


def transposed_left(left, right):
    return lax.dot_general(
        left, right, (((0,), (0,)), ((), ())), preferred_element_type=jnp.float32
    )


def transposed_right(left, right):
    return lax.dot_general(
        left, right, (((1,), (1,)), ((), ())), preferred_element_type=jnp.float32
    )


def layer_norm(summed, gain, shift):
    center = summed - jnp.mean(summed, axis=-1, keepdims=True)
    spread = jnp.mean(center * center, axis=-1, keepdims=True)
    return center * lax.rsqrt(spread + 1e-05) * gain + shift


def exact_gelu(values):
    return jax.nn.gelu(values, approximate=False)


def per_device(
    tokens,
    segments,
    padding,
    query_weight,
    query_bias,
    key_weight,
    value_weight,
    value_bias,
    output_weight,
    output_bias,
    first_gain,
    first_shift,
    inner_weight,
    inner_bias,
    outer_weight,
    outer_bias,
    second_gain,
    second_shift,
    cotangent,
):
    gathered = (
        lax.all_gather(query_weight, ("dp", "seq"), axis=0, tiled=True),
        lax.all_gather(query_bias, ("dp", "seq"), axis=0, tiled=True),
        lax.all_gather(key_weight, ("dp", "seq"), axis=0, tiled=True),
        lax.all_gather(value_weight, ("dp", "seq"), axis=0, tiled=True),
        lax.all_gather(value_bias, ("dp", "seq"), axis=0, tiled=True),
        lax.all_gather(output_weight, ("dp", "seq"), axis=0, tiled=True),
        lax.all_gather(output_bias, ("dp", "seq"), axis=0, tiled=True),
        lax.all_gather(first_gain, ("dp", "seq"), axis=0, tiled=True),
        lax.all_gather(first_shift, ("dp", "seq"), axis=0, tiled=True),
        lax.all_gather(inner_weight, ("dp", "seq"), axis=0, tiled=True),
        lax.all_gather(inner_bias, ("dp", "seq"), axis=0, tiled=True),
        lax.all_gather(outer_weight, ("dp", "seq"), axis=0, tiled=True),
        lax.all_gather(outer_bias, ("dp", "seq"), axis=0, tiled=True),
        lax.all_gather(second_gain, ("dp", "seq"), axis=0, tiled=True),
        lax.all_gather(second_shift, ("dp", "seq"), axis=0, tiled=True),
    )
    (
        query_matrix,
        query_vector,
        key_matrix,
        value_matrix,
        value_vector,
        output_matrix,
        output_vector,
        gain_first,
        shift_first,
        inner_matrix,
        inner_vector,
        outer_matrix,
        outer_vector,
        gain_second,
        shift_second,
    ) = gathered
    gain_first = gain_first.astype(jnp.float32)
    shift_first = shift_first.astype(jnp.float32)
    gain_second = gain_second.astype(jnp.float32)
    shift_second = shift_second.astype(jnp.float32)
    count_seq, block_len, features = tokens.shape
    offset = lax.axis_index("seq") * block_len
    token_rows = tokens.reshape(count_seq * block_len, features)
    token_low = token_rows.astype(jnp.bfloat16)
    queries = (
        (matmul(token_low, query_matrix) + query_vector.astype(jnp.float32))
        .astype(jnp.bfloat16)
        .reshape(count_seq, block_len, features)
    )
    keys_local = (
        matmul(token_low, key_matrix).astype(jnp.bfloat16).reshape(count_seq, block_len, features)
    )
    values_local = (
        (matmul(token_low, value_matrix) + value_vector.astype(jnp.float32))
        .astype(jnp.bfloat16)
        .reshape(count_seq, block_len, features)
    )
    keys_all, values_all = (
        lax.all_gather(keys_local, "seq", axis=1, tiled=True),
        lax.all_gather(values_local, "seq", axis=1, tiled=True),
    )
    query_segment = lax.dynamic_slice_in_dim(segments, offset, block_len, 1)
    query_padding = lax.dynamic_slice_in_dim(padding, offset, block_len, 1)
    allowed = (query_segment[:, :, None] == segments[:, None, :]) & (
        (padding[:, None, :] == 1) | (query_padding[:, :, None] == 0)
    )

    def head_slices(head_index):
        column = head_index * HEAD_DIM
        query_head = lax.dynamic_slice_in_dim(queries, column, HEAD_DIM, 2)
        key_head = lax.dynamic_slice_in_dim(keys_all, column, HEAD_DIM, 2)
        value_head = lax.dynamic_slice_in_dim(values_all, column, HEAD_DIM, 2)
        scores = (
            jnp.einsum("sqd,skd->sqk", query_head, key_head, preferred_element_type=jnp.float32)
            * 0.125
        )
        scores = jnp.where(allowed, scores, neg_big)
        return (column, query_head, key_head, value_head, scores)

    def forward_head(head_index, carry):
        mixed, logsum = carry
        column, query_head, key_head, value_head, scores = head_slices(head_index)
        row_max = jnp.max(scores, axis=2, keepdims=True)
        exponent = jnp.exp(scores - row_max)
        row_total = jnp.sum(exponent, axis=2, keepdims=True)
        probs_low = (exponent / row_total).astype(jnp.bfloat16)
        head_part = jnp.einsum(
            "sqk,skd->sqd", probs_low, value_head, preferred_element_type=jnp.float32
        ).astype(jnp.bfloat16)
        mixed = lax.dynamic_update_slice_in_dim(mixed, head_part, column, 2)
        logsum = lax.dynamic_update_index_in_dim(
            logsum, (row_max + jnp.log(row_total))[:, :, 0], head_index, 0
        )
        return (mixed, logsum)

    mixed, logsum = lax.fori_loop(
        0,
        HEADS,
        forward_head,
        (
            jnp.zeros((count_seq, block_len, features), jnp.bfloat16),
            jnp.zeros((HEADS, count_seq, block_len), jnp.float32),
        ),
    )
    mixed_rows = mixed.reshape(count_seq * block_len, features)
    first_sum = token_rows + matmul(mixed_rows, output_matrix) + output_vector.astype(jnp.float32)
    hidden, first_pull = jax.vjp(layer_norm, first_sum, gain_first, shift_first)
    hidden_low = hidden.astype(jnp.bfloat16)
    inner = matmul(hidden_low, inner_matrix) + inner_vector.astype(jnp.float32)
    activation, gelu_pull = jax.vjp(exact_gelu, inner)
    activation_low = activation.astype(jnp.bfloat16)
    second_sum = hidden + matmul(activation_low, outer_matrix) + outer_vector.astype(jnp.float32)
    layer_output, second_pull = jax.vjp(layer_norm, second_sum, gain_second, shift_second)
    again = (
        lax.all_gather(query_weight, ("dp", "seq"), axis=0, tiled=True),
        lax.all_gather(key_weight, ("dp", "seq"), axis=0, tiled=True),
        lax.all_gather(value_weight, ("dp", "seq"), axis=0, tiled=True),
        lax.all_gather(output_weight, ("dp", "seq"), axis=0, tiled=True),
        lax.all_gather(inner_weight, ("dp", "seq"), axis=0, tiled=True),
        lax.all_gather(outer_weight, ("dp", "seq"), axis=0, tiled=True),
    )
    again_query, again_key, again_value, again_output, again_inner, again_outer = again
    second_back, second_gains, second_shifts = second_pull(
        cotangent.reshape(count_seq * block_len, features)
    )
    outer_low = second_back.astype(jnp.bfloat16)
    outer_delta = transposed_left(activation_low, outer_low)
    inner_back = gelu_pull(transposed_right(outer_low, again_outer))[0].astype(jnp.bfloat16)
    inner_delta = transposed_left(hidden_low, inner_back)
    hidden_back = transposed_right(inner_back, again_inner) + second_back
    first_back, first_gains, first_shifts = first_pull(hidden_back)
    branch_low = first_back.astype(jnp.bfloat16)
    output_delta = transposed_left(mixed_rows, branch_low)
    mixed_back = (
        transposed_right(branch_low, again_output)
        .astype(jnp.bfloat16)
        .reshape(count_seq, block_len, features)
    )
    total_len = segments.shape[1]

    def backward_head(head_index, carry):
        query_acc, key_acc, value_acc = carry
        column, query_head, key_head, value_head, scores = head_slices(head_index)
        grad_head = lax.dynamic_slice_in_dim(mixed_back, column, HEAD_DIM, 2)
        row_log = lax.dynamic_index_in_dim(logsum, head_index, 0, keepdims=False)
        probs = jnp.exp(scores - row_log[:, :, None])
        value_part = jnp.einsum(
            "sqk,sqd->skd",
            probs.astype(jnp.bfloat16),
            grad_head,
            preferred_element_type=jnp.float32,
        )
        prob_back = jnp.einsum(
            "sqd,skd->sqk", grad_head, value_head, preferred_element_type=jnp.float32
        )
        score_back = (
            probs * (prob_back - jnp.sum(probs * prob_back, axis=2, keepdims=True))
        ).astype(jnp.bfloat16)
        query_part = (
            jnp.einsum("sqk,skd->sqd", score_back, key_head, preferred_element_type=jnp.float32)
            * 0.125
        )
        key_part = (
            jnp.einsum("sqk,sqd->skd", score_back, query_head, preferred_element_type=jnp.float32)
            * 0.125
        )
        query_acc = lax.dynamic_update_slice_in_dim(query_acc, query_part, column, 2)
        key_acc = lax.dynamic_update_slice_in_dim(key_acc, key_part, column, 2)
        value_acc = lax.dynamic_update_slice_in_dim(value_acc, value_part, column, 2)
        return (query_acc, key_acc, value_acc)

    query_acc, key_acc, value_acc = lax.fori_loop(
        0,
        HEADS,
        backward_head,
        (
            jnp.zeros((count_seq, block_len, features), jnp.float32),
            jnp.zeros((count_seq, total_len, features), jnp.float32),
            jnp.zeros((count_seq, total_len, features), jnp.float32),
        ),
    )
    key_sum, value_sum = (
        lax.psum_scatter(
            key_acc.astype(jnp.bfloat16), "seq", scatter_dimension=1, tiled=True
        ).astype(jnp.float32),
        lax.psum_scatter(
            value_acc.astype(jnp.bfloat16), "seq", scatter_dimension=1, tiled=True
        ).astype(jnp.float32),
    )
    query_low = query_acc.reshape(count_seq * block_len, features).astype(jnp.bfloat16)
    key_low = key_sum.reshape(count_seq * block_len, features).astype(jnp.bfloat16)
    value_low = value_sum.reshape(count_seq * block_len, features).astype(jnp.bfloat16)
    query_delta = transposed_left(token_low, query_low)
    key_delta = transposed_left(token_low, key_low)
    value_delta = transposed_left(token_low, value_low)
    input_back = (
        transposed_right(query_low, again_query)
        + transposed_right(key_low, again_key)
        + transposed_right(value_low, again_value)
        + first_back
    )
    shards = (
        lax.psum_scatter(query_delta, ("dp", "seq"), scatter_dimension=0, tiled=True),
        lax.psum_scatter(
            jnp.sum(query_low.astype(jnp.float32), axis=0),
            ("dp", "seq"),
            scatter_dimension=0,
            tiled=True,
        ),
        lax.psum_scatter(key_delta, ("dp", "seq"), scatter_dimension=0, tiled=True),
        lax.psum_scatter(value_delta, ("dp", "seq"), scatter_dimension=0, tiled=True),
        lax.psum_scatter(
            jnp.sum(value_low.astype(jnp.float32), axis=0),
            ("dp", "seq"),
            scatter_dimension=0,
            tiled=True,
        ),
        lax.psum_scatter(output_delta, ("dp", "seq"), scatter_dimension=0, tiled=True),
        lax.psum_scatter(
            jnp.sum(branch_low.astype(jnp.float32), axis=0),
            ("dp", "seq"),
            scatter_dimension=0,
            tiled=True,
        ),
        lax.psum_scatter(first_gains, ("dp", "seq"), scatter_dimension=0, tiled=True),
        lax.psum_scatter(first_shifts, ("dp", "seq"), scatter_dimension=0, tiled=True),
        lax.psum_scatter(inner_delta, ("dp", "seq"), scatter_dimension=0, tiled=True),
        lax.psum_scatter(
            jnp.sum(inner_back.astype(jnp.float32), axis=0),
            ("dp", "seq"),
            scatter_dimension=0,
            tiled=True,
        ),
        lax.psum_scatter(outer_delta, ("dp", "seq"), scatter_dimension=0, tiled=True),
        lax.psum_scatter(
            jnp.sum(outer_low.astype(jnp.float32), axis=0),
            ("dp", "seq"),
            scatter_dimension=0,
            tiled=True,
        ),
        lax.psum_scatter(second_gains, ("dp", "seq"), scatter_dimension=0, tiled=True),
        lax.psum_scatter(second_shifts, ("dp", "seq"), scatter_dimension=0, tiled=True),
    )
    return (
        layer_output.reshape(tokens.shape),
        input_back.reshape(tokens.shape),
        shards[0],
        shards[1],
        shards[2],
        shards[3],
        shards[4],
        shards[5],
        shards[6],
        shards[7],
        shards[8],
        shards[9],
        shards[10],
        shards[11],
        shards[12],
        shards[13],
        shards[14],
    )


def solution(mesh):
    placed = (
        P("dp", "seq", None),
        P("dp", None),
        P("dp", None),
        P(("dp", "seq"), None),
        P(("dp", "seq")),
        P(("dp", "seq"), None),
        P(("dp", "seq"), None),
        P(("dp", "seq")),
        P(("dp", "seq"), None),
        P(("dp", "seq")),
        P(("dp", "seq")),
        P(("dp", "seq")),
        P(("dp", "seq"), None),
        P(("dp", "seq")),
        P(("dp", "seq"), None),
        P(("dp", "seq")),
        P(("dp", "seq")),
        P(("dp", "seq")),
        P("dp", "seq", None),
    )
    return jax.shard_map(
        per_device,
        mesh=mesh,
        in_specs=placed,
        out_specs=(
            P("dp", "seq", None),
            P("dp", "seq", None),
            P(("dp", "seq"), None),
            P(("dp", "seq")),
            P(("dp", "seq"), None),
            P(("dp", "seq"), None),
            P(("dp", "seq")),
            P(("dp", "seq"), None),
            P(("dp", "seq")),
            P(("dp", "seq")),
            P(("dp", "seq")),
            P(("dp", "seq"), None),
            P(("dp", "seq")),
            P(("dp", "seq"), None),
            P(("dp", "seq")),
            P(("dp", "seq")),
            P(("dp", "seq")),
        ),
        check_vma=False,
    )
```

profile of v0, /device:TPU:0, one launch (start us, length us, event | category | flops | bytes accessed | tf_op | source)
XLA Modules:
  0.0 1472.6 jit_solution(16439067446823279791)
XLA Ops:
  17.0 42.5 %all-reduce.19 = (bf16[768]{0:T(1024)(128)(2,1)S(1)}, bf16[768]{0:T(1024)(128)(2,1)S(1)}, bf16[768]{0:T(1024)(128)(2,1)S(1)}, bf16[768]{0:T(1024)(128)(2,1)S(1)}...) all-reduce(bf16[768]{0:T(1024)(128)(2,1)S(1)} %dynamic-update-slice, ...), channel_id=1, replica_groups=mesh['dp'=16,'seq'=2] {'dp','seq'}, use_global_device_ids=true, to_apply=%add | all-reduce | flops 9216 | bytes 36864
  72.4 51.4 %all-gather.11.cloned.1.call-done = bf16[768,768]{1,0:T(8,128)(2,1)} async-done(((bf16[24,768]{1,0:T(8,128)(2,1)}), bf16[768,768]{1,0:T(8,128)(2,1)}) %all-gather.11.cloned.1.call-update) | async-done | bytes 1179664 | tf_op jit(solution)/shard_map/all_gather | solution.py:63
  131.6 48.2 %all-gather.9.cloned.1.call-done = bf16[768,768]{1,0:T(8,128)(2,1)} async-done(((bf16[24,768]{1,0:T(8,128)(2,1)}), bf16[768,768]{1,0:T(8,128)(2,1)}) %all-gather.9.cloned.1.call-update) | async-done | bytes 1179664 | tf_op jit(solution)/shard_map/all_gather | solution.py:61
  183.6 42.0 %all-gather.17.cloned.1.call-done = bf16[2,1024,768]{1,2,0:T(8,128)(2,1)} async-done(((bf16[2,512,768]{1,2,0:T(8,128)(2,1)}), bf16[2,1024,768]{1,2,0:T(8,128)(2,1)}) %all-gather.17.cloned.1.call-update) | async-done | bytes 3145744 | tf_op jit(solution)/shard_map/all_gather | solution.py:117
  225.6 46.9 %all-gather.13.cloned.1.call-done = bf16[2,1024,768]{1,2,0:T(8,128)(2,1)} async-done(((bf16[2,512,768]{1,2,0:T(8,128)(2,1)}), bf16[2,1024,768]{1,2,0:T(8,128)(2,1)}) %all-gather.13.cloned.1.call-update) | async-done | bytes 3145744 | tf_op jit(solution)/shard_map/all_gather | solution.py:116
  272.6 75.9 %while.34 = (s32[]{:T(128)}, bf16[2,512,768]{1,2,0:T(8,128)(2,1)S(1)}, f32[12,2,512]{2,1,0:T(2,128)}, bf16[2,512,768]{1,2,0:T(8,128)(2,1)S(1)}, bf16[2,1024,768]...) while((s32[]{:T(128)}, ...), condition=%wide.region_3.4_spmd.clone, body=%wide.region_0.3_spmd.clone.sunk | while | flops 280034304 | bytes 13423283 | solution.py:153
  354.9 40.0 %all-gather.21.cloned.1.call-done = bf16[768,3072]{1,0:T(8,128)(2,1)} async-done(((bf16[24,3072]{1,0:T(8,128)(2,1)}), bf16[768,3072]{1,0:T(8,128)(2,1)}) %all-gather.21.cloned.1.call-update) | async-done | bytes 4718608 | tf_op jit(solution)/shard_map/all_gather | solution.py:70
  394.9 35.8 %multiply_convert_fusion.1 = (bf16[1024,3072]{1,0:T(8,128)(2,1)}, f32[1024,3072]{1,0:T(8,128)}, f32[1024,3072]{1,0:T(8,128)}) fusion(f32[3072]{0:T(1024)S(1)} %convert_element_type.144, bf16[768,3072]{1,0:T(8,128)(2,1)} %all-gather.21.cloned.1.call-done, f32[1024,768]{1,0:T(8,128)S(1)} %get-tuple-element.581, f32[768]{0:T(1024)S(1)} %convert_element_type.142, ...), kind=kOutput, calls=%fused_computation.43 | convolution fusion | flops 5043388416 | bytes 39348224 | tf_op jit(solution)/shard_map/dot_general | solution.py:14
  430.8 29.0 %all-gather.23.cloned.1.call-done = bf16[3072,768]{1,0:T(8,128)(2,1)} async-done(((bf16[96,768]{1,0:T(8,128)(2,1)}), bf16[3072,768]{1,0:T(8,128)(2,1)}) %all-gather.23.cloned.1.call-update) | async-done | bytes 4718608 | tf_op jit(solution)/shard_map/all_gather | solution.py:72
  459.8 9.0 fusion.56
  477.4 18.2 %convert_reduce_fusion = (f32[3072]{0:T(1024)S(1)}, bf16[1024,3072]{1,0:T(8,128)(2,1)}) fusion(f32[1024,3072]{1,0:T(8,128)} %get-tuple-element.574, bf16[1024,768]{1,0:T(8,128)(2,1)} %get-tuple-element.566, bf16[3072,768]{1,0:T(8,128)(2,1)} %all-gather.23.cloned.1.call-done, f32[1024,3072]{1,0:T(8,128)} %get-tuple-element.582, ...), kind=kOutput, calls=%fused_computation.41 | convolution fusion | flops 4885312512 | bytes 37773312 | tf_op jit(solution)/shard_map/dot_general | solution.py:24
  495.6 9.5 multiply_reduce_fusion.1
  519.4 151.2 %while.35 = (s32[]{:T(128)}, bf16[2,512,768]{1,2,0:T(8,128)(2,1)}, bf16[2,1024,768]{1,2,0:T(8,128)(2,1)}, bf16[2,1024,768]{1,2,0:T(8,128)(2,1)}, bf16[2,512,768]...) while((s32[]{:T(128)}, bf16[2,512,768]{1,2,0:T(8,128)(2,1)}, ...), condition=%wide.region_14.15_spmd.clone, body=%wide.region_12.14_spmd.clone.sunk | while | flops 683867136 | bytes 34119888 | solution.py:229
  696.2 21.0 %reduce-scatter.15.cloned.1.call-done = bf16[2,512,768]{2,1,0:T(8,128)(2,1)} async-done(((bf16[2,1024,768]{2,1,0:T(8,128)(2,1)}), bf16[2,512,768]{2,1,0:T(8,128)(2,1)}) %reduce-scatter.15.cloned.1.call-update) | async-done | bytes 1572880 | tf_op jit(solution)/shard_map/reduce_scatter | solution.py:240
  725.5 37.8 %reduce-scatter.17.cloned.1.call-done = bf16[2,512,768]{2,1,0:T(8,128)(2,1)} async-done(((bf16[2,1024,768]{2,1,0:T(8,128)(2,1)}), bf16[2,512,768]{2,1,0:T(8,128)(2,1)}) %reduce-scatter.17.cloned.1.call-update) | async-done | bytes 1572880 | tf_op jit(solution)/shard_map/reduce_scatter | solution.py:243
  771.9 10.7 fusion.47
  784.0 10.2 fusion.60
  803.5 40.2 %all-reduce.18 = (f32[768]{0:T(1024)S(1)}, f32[768]{0:T(1024)S(1)}, f32[768]{0:T(1024)S(1)}, f32[768]{0:T(1024)S(1)}, f32[768]{0:T(1024)S(1)}, /*index=5*/f32[30...) all-reduce(f32[768]{0:T(1024)S(1)} %convert_reduce_fusion.4, ...), channel_id=5, replica_groups=mesh['dp'=16,'seq'=2] {'dp','seq'}, use_global_device_ids=true, to_apply=%region_19.20.clone | all-reduce | flops 9216 | bytes 73728
  855.7 13.2 reduce-scatter.19.cloned.1.call-done
  868.9 104.4 %reduce-scatter.25.cloned.1.call-done = f32[24,768]{1,0:T(8,128)} async-done(((f32[768,768]{1,0:T(8,128)}), f32[24,768]{1,0:T(8,128)}) %reduce-scatter.25.cloned.1.call-update) | async-done | bytes 73744
  973.3 104.4 %reduce-scatter.27.cloned.1.call-done = f32[24,768]{1,0:T(8,128)} async-done(((f32[768,768]{1,0:T(8,128)}), f32[24,768]{1,0:T(8,128)}) %reduce-scatter.27.cloned.1.call-update) | async-done | bytes 73744
  1077.7 104.3 %reduce-scatter.29.cloned.1.call-done = f32[24,768]{1,0:T(8,128)} async-done(((f32[768,768]{1,0:T(8,128)}), f32[24,768]{1,0:T(8,128)}) %reduce-scatter.29.cloned.1.call-update) | async-done | bytes 73744
  1182.0 141.9 %reduce-scatter.21.cloned.1.call-done = f32[24,3072]{1,0:T(8,128)} async-done(((f32[768,3072]{1,0:T(8,128)}), f32[24,3072]{1,0:T(8,128)}) %reduce-scatter.21.cloned.1.call-update) | async-done | bytes 294928 | tf_op jit(solution)/shard_map/reduce_scatter | solution.py:284
  1323.9 141.8 %reduce-scatter.23.cloned.1.call-done = f32[96,768]{1,0:T(8,128)} async-done(((f32[3072,768]{1,0:T(8,128)}), f32[96,768]{1,0:T(8,128)}) %reduce-scatter.23.cloned.1.call-update) | async-done | bytes 294928 | tf_op jit(solution)/shard_map/reduce_scatter | solution.py:291
  (302 shorter events, 354.6 us)
Async XLA Ops:
  7.2 60.9 %all-gather.15.cloned.1.call-start = ((), (), s32[]{:S(2)}) async-start(), calls=%async_computation.11 | async-start | bytes 1216512 | tf_op jit(solution)/shard_map/all_gather | solution.py:64
  7.9 115.9 %all-gather.11.cloned.1.call-start = ((), (), s32[]{:S(2)}) async-start(), calls=%async_computation.9 | async-start | bytes 1216512 | tf_op jit(solution)/shard_map/all_gather | solution.py:63
  8.7 171.1 %all-gather.9.cloned.1.call-start = ((), (), s32[]{:S(2)}) async-start(), calls=%async_computation.8 | async-start | bytes 1216512 | tf_op jit(solution)/shard_map/all_gather | solution.py:61
  9.4 216.2 %all-gather.17.cloned.1.call-start = ((), (), s32[]{:S(2)}) async-start(), calls=%async_computation.12 | async-start | bytes 4718592 | tf_op jit(solution)/shard_map/all_gather | solution.py:117
  72.4 200.1 %all-gather.13.cloned.1.call-start = ((), (), s32[]{:S(2)}) async-start(), calls=%async_computation.10 | async-start | bytes 4718592 | tf_op jit(solution)/shard_map/all_gather | solution.py:116
  128.1 222.0 %all-gather.19.cloned.1.call-start = ((), (), s32[]{:S(2)}) async-start(), calls=%async_computation.13 | async-start | bytes 1216512 | tf_op jit(solution)/shard_map/all_gather | solution.py:66
  128.7 266.2 %all-gather.21.cloned.1.call-start = ((), (), s32[]{:S(2)}) async-start(), calls=%async_computation.14 | async-start | bytes 4866048 | tf_op jit(solution)/shard_map/all_gather | solution.py:70
  129.5 330.3 %all-gather.23.cloned.1.call-start = ((), (), s32[]{:S(2)}) async-start(), calls=%async_computation.15 | async-start | bytes 4866048 | tf_op jit(solution)/shard_map/all_gather | solution.py:72
  130.2 587.0 %reduce-scatter.15.cloned.1.call-start = ((), (), s32[]{:S(2)}) async-start(), calls=%async_computation.16 | async-start | bytes 4718592 | tf_op jit(solution)/shard_map/reduce_scatter | solution.py:240
  348.5 5.9 copy-start.15
  348.5 5.9 copy-start.17
  348.5 5.9 copy-start.21
  506.6 4.7 copy-start.2
  675.3 88.0 %reduce-scatter.17.cloned.1.call-start = ((), (), s32[]{:S(2)}) async-start(), calls=%async_computation.17 | async-start | bytes 4718592 | tf_op jit(solution)/shard_map/reduce_scatter | solution.py:243
  680.0 188.9 %reduce-scatter.19.cloned.1.call-start = ((), (), s32[]{:S(2)}) async-start(), calls=%async_computation.18 | async-start | bytes 2433024 | tf_op jit(solution)/shard_map/reduce_scatter | solution.py:275
  685.1 288.2 %reduce-scatter.25.cloned.1.call-start = ((), (), s32[]{:S(2)}) async-start(), calls=%async_computation.21 | async-start | bytes 2433024
  696.1 381.6 %reduce-scatter.27.cloned.1.call-start = ((), (), s32[]{:S(2)}) async-start(), calls=%async_computation.22 | async-start | bytes 2433024
  725.5 456.5 %reduce-scatter.29.cloned.1.call-start = ((), (), s32[]{:S(2)}) async-start(), calls=%async_computation.23 | async-start | bytes 2433024
  771.9 552.0 %reduce-scatter.21.cloned.1.call-start = ((), (), s32[]{:S(2)}) async-start(), calls=%async_computation.19 | async-start | bytes 9732096 | tf_op jit(solution)/shard_map/reduce_scatter | solution.py:284
  782.6 683.1 %reduce-scatter.23.cloned.1.call-start = ((), (), s32[]{:S(2)}) async-start(), calls=%async_computation.20 | async-start | bytes 9732096 | tf_op jit(solution)/shard_map/reduce_scatter | solution.py:291
  798.1 5.0 copy-start.4
  798.1 5.3 copy-start.13
  798.2 5.3 copy-start.14
  798.2 50.8 %copy-start.23 = (bf16[768,768]{1,0:T(8,128)(2,1)S(1)}, bf16[768,768]{1,0:T(8,128)(2,1)}, u32[]{:S(2)}) copy-start(bf16[768,768]{1,0:T(8,128)(2,1)} %all-gather.11.cloned.1.call-done) | copy-start | bytes 3538948
  (17 other events, 47.8 us)
Sparse Core Ops, SparseCore 0:
  10.9 57.1 all-gather.14
  71.0 52.7 all-gather.10
  126.8 52.9 all-gather.8
  181.7 43.7 all-gather.16
  227.5 44.8 all-gather.12
  275.2 54.0 all-gather.18
  332.3 62.6 all-gather.20
  397.8 61.9 all-gather.22
  675.4 41.7 reduce-scatter.14
  719.8 43.4 reduce-scatter.16
  769.2 99.6 reduce-scatter.18
  874.6 98.6 reduce-scatter.24
  979.1 98.4 reduce-scatter.26
  1083.4 98.5 reduce-scatter.28
  1188.3 135.5 reduce-scatter.20
  1330.2 135.4 reduce-scatter.22
where the time goes:
time: 1480 us; the launch traced here: 1470 us
  waiting for transfers between devices  937 us (63%)
  matrix products  332 us (22%)
  blocking collectives  82.7 us (6%)
  local copies, waits for them, and re-layouts  63.7 us (4%)
  other arithmetic  40.8 us (3%)
  between operations  14.9 us (1%)
    unnamed x19, waiting for transfers between devices  317 us
    reduce_scatter x1, waiting for transfers between devices, per_device(): lax.psum_scatter(inner_delta, ('dp', 'seq'), scatter_dimension=0, tiled=T...  142 us
    reduce_scatter x1, waiting for transfers between devices, per_device(): lax.psum_scatter(outer_delta, ('dp', 'seq'), scatter_dimension=0, tiled=T...  142 us
    unnamed x2, blocking collectives  82.7 us
    dot_general x24, matrix products, head_slices(): jnp.einsum('sqd,skd->sqk', query_head, key_head, preferred_element_type=j...  68 us
    dot_general x6, matrix products, matmul(): return jnp.dot(left, right, preferred_element_type=jnp.float32)  57 us
    all_gather x1, waiting for transfers between devices, per_device(): lax.all_gather(key_weight, ('dp', 'seq'), axis=0, tiled=True)  51.4 us
    all_gather x1, waiting for transfers between devices, per_device(): lax.all_gather(query_weight, ('dp', 'seq'), axis=0, tiled=True)  48.2 us
  transfers between devices with their start and end apart: 16, of which 15 were waited for; matrix products, arithmetic and copies ran while one was open for 15% of the time, Pallas kernels for 0%

commit v1 on v0

--- a/solution.py
+++ b/solution.py
@@ -1,6 +1,10 @@
+import functools
+
 import jax
 import jax.numpy as jnp
 from jax import lax
+from jax.experimental import pallas as pl
+from jax.experimental.pallas import tpu as pltpu
 from jax.sharding import PartitionSpec as P
 
 HEADS = 12
@@ -36,7 +40,7 @@
     return jax.nn.gelu(values, approximate=False)
 
 
-def per_device(
+def gathered_layer(
     tokens,
     segments,
     padding,
@@ -319,6 +323,691 @@
     )
 
 
+MESH = pl.DeviceIdType.MESH
+BF = jnp.bfloat16
+F32 = jnp.float32
+LOG2E = 1.4426950408889634
+SCORE_SCALE = 0.125 * LOG2E
+VMEM_MOST = 66 * 1024 * 1000
+BLOCK = 256
+
+
+def grid_dims(mesh):
+    return (mesh.shape["dp"] // 4, 2, 2, mesh.shape["seq"])
+
+
+def swappable(mesh, shape):
+    count, rows, features = shape
+    return (
+        mesh.shape["seq"] == 2
+        and count == 2
+        and mesh.shape["dp"] % 4 == 0
+        and rows % (2 * BLOCK) == 0
+        and features % 128 == 0
+    )
+
+
+class Place:
+    def __init__(self, dims):
+        self.dims = dims
+        nz, nx, nc, ny = dims
+        dp, y = lax.axis_index("dp"), lax.axis_index("seq")
+        z, x, c = dp // (nx * nc), (dp // nc) % nx, dp % nc
+        self.z, self.x, self.c, self.y = z, x, c, y
+        self.xo, self.co, self.yo = 1 - x, 1 - c, 1 - y
+        self.along_z = [self.device(lax.rem(z + d, nz), x, c, y) for d in range(1, nz)]
+        self.along_x = self.device(z, self.xo, c, y)
+        self.along_c = self.device(z, x, self.co, y)
+        self.along_y = self.device(z, x, c, self.yo)
+
+    def device(self, z, x, c, y):
+        nz, nx, nc, ny = self.dims
+        return ((z * nx + x) * nc + c, y)
+
+    def greet(self):
+        barrier = pltpu.get_barrier_semaphore()
+        self.partners = self.along_z + [self.along_x, self.along_c, self.along_y]
+        for partner in self.partners:
+            pl.semaphore_signal(barrier, inc=1, device_id=partner, device_id_type=MESH)
+
+    def meet(self):
+        pl.semaphore_wait(pltpu.get_barrier_semaphore(), len(self.partners))
+
+
+def remote(src, dst, send, recv, device):
+    return pltpu.make_async_remote_copy(
+        src_ref=src, dst_ref=dst, send_sem=send, recv_sem=recv, device_id=device, device_id_type=MESH
+    )
+
+
+def halves(width):
+    part = width // 256 * 128
+    return pl.ds(0, part), pl.ds(part, width - part)
+
+
+def gather_kernel(dims, count, *refs):
+    nz = dims[0]
+    ins, (tokens, cotangent) = refs[:count], refs[count : count + 2]
+    outs, (low_out, cot_out) = refs[count + 2 : 2 * count + 2], refs[2 * count + 2 : 2 * count + 4]
+    own_t, other_t, other_c, low, low_c = refs[2 * count + 4 : 2 * count + 9]
+    local, zs, zr, ps, pr, qs, qr, cs, cr, ts, tr = refs[2 * count + 9 :]
+    at = Place(dims)
+    z, x, c, y = at.z, at.x, at.c, at.y
+    loads = [
+        pltpu.make_async_copy(tokens.at[at.yo], other_t, local.at[count]),
+        pltpu.make_async_copy(tokens.at[y], own_t, local.at[count + 1]),
+        pltpu.make_async_copy(cotangent.at[at.yo], other_c, local.at[count + 2]),
+    ]
+    for load in loads:
+        load.start()
+    at.greet()
+    loads[0].wait()
+    low[1] = other_t[...].astype(BF)
+    at.meet()
+    own, along = [], []
+    for i in range(count):
+        copy = pltpu.make_async_copy(ins[i], outs[i].at[z, x, c, y], local.at[i])
+        copy.start()
+        own.append(copy)
+        row = []
+        for d in range(1, nz):
+            k = remote(ins[i], outs[i].at[z, x, c, y], zs.at[i, d - 1], zr.at[i, d - 1], at.along_z[d - 1])
+            k.start()
+            row.append(k)
+        along.append(row)
+    swap = remote(low.at[1], low_out.at[1], ts.at[0], tr.at[0], at.along_y)
+    swap.start()
+    loads[1].wait()
+    low[0] = own_t[...].astype(BF)
+    loads[2].wait()
+    low_c[...] = other_c[...].astype(BF)
+    keep = pltpu.make_async_copy(low.at[0], low_out.at[0], local.at[count + 3])
+    keep.start()
+    second, third, fourth = [None] * count, [None] * count, [None] * count
+
+    def spread(i):
+        own[i].wait()
+        for k in along[i]:
+            k.wait()
+        a, b = halves(ins[i].shape[1])
+        a, b = outs[i].at[:, x, c, y, :, a], outs[i].at[:, x, c, y, :, b]
+        second[i] = (
+            remote(a, a, ps.at[i, 0], pr.at[i, 0], at.along_x),
+            remote(b, b, ps.at[i, 1], pr.at[i, 1], at.along_y),
+        )
+        for k in second[i]:
+            k.start()
+
+    def spread_again(i):
+        for k in second[i]:
+            k.wait()
+        a, b = halves(ins[i].shape[1])
+        a, b = outs[i].at[:, :, c, y, :, a], outs[i].at[:, x, c, :, :, b]
+        third[i] = (
+            remote(a, a, qs.at[i, 0], qr.at[i, 0], at.along_y),
+            remote(b, b, qs.at[i, 1], qr.at[i, 1], at.along_x),
+        )
+        for k in third[i]:
+            k.start()
+
+    def share(i):
+        for k in third[i]:
+            k.wait()
+        a = outs[i].at[:, :, c]
+        fourth[i] = remote(a, a, cs.at[i], cr.at[i], at.along_c)
+        fourth[i].start()
+
+    swap_c = remote(low_c, cot_out, ts.at[1], tr.at[1], at.along_y)
+    for t in range(count + 2):
+        if t < count:
+            spread(t)
+        if 0 <= t - 1 < count:
+            spread_again(t - 1)
+        if t == count - 1:
+            swap_c.start()
+        if 0 <= t - 2 < count:
+            share(t - 2)
+    for k in fourth:
+        k.wait()
+    swap.wait()
+    swap_c.wait()
+    keep.wait()
+
+
+def gather(dims, shards, tokens, cotangent):
+    nz = dims[0]
+    n = len(shards)
+    rows, d = tokens.shape[1:]
+    hbm, vmem = pl.BlockSpec(memory_space=pl.ANY), pl.BlockSpec(memory_space=pltpu.VMEM)
+    sem = pltpu.SemaphoreType.DMA
+    out = [jax.ShapeDtypeStruct(dims + s.shape, s.dtype) for s in shards]
+    out += [jax.ShapeDtypeStruct((2, rows, d), BF), jax.ShapeDtypeStruct((rows, d), BF)]
+    return pl.pallas_call(
+        functools.partial(gather_kernel, dims, n),
+        out_shape=out,
+        in_specs=[vmem] * n + [hbm] * 2,
+        out_specs=[hbm] * (n + 2),
+        scratch_shapes=[pltpu.VMEM((rows, d), F32)] * 3
+        + [pltpu.VMEM((2, rows, d), BF), pltpu.VMEM((rows, d), BF)]
+        + [sem((n + 4,)), sem((n, nz - 1)), sem((n, nz - 1))]
+        + [sem((n, 2))] * 4
+        + [sem((n,))] * 2
+        + [sem((2,))] * 2,
+        compiler_params=pltpu.CompilerParams(collective_id=0, has_side_effects=True),
+        name="gather",
+    )(*shards, tokens, cotangent)
+
+
+def scatter_kernel(dims, count, *refs):
+    nz, nx, nc, ny = dims
+    ins, vec, swaps = refs[:count], refs[count], refs[count + 1 : count + 3]
+    outs, vec_out = refs[count + 3 : 2 * count + 3], refs[2 * count + 3]
+    swap_outs = refs[2 * count + 4 : 2 * count + 6]
+    rest = list(refs[2 * count + 6 :])
+    m0, r0, r1, r2, r3 = (rest[k * count : (k + 1) * count] for k in range(5))
+    vm, vc, vx, vy, vz = rest[5 * count : 5 * count + 5]
+    local, s0, q0, s1, q1, s2, q2, s3, q3, vs, vq, ws, wq = rest[5 * count + 5 :]
+    at = Place(dims)
+    z, x, c, y = at.z, at.x, at.c, at.y
+    at.greet()
+    loads = []
+    for i in range(count):
+        k = pltpu.make_async_copy(ins[i].at[:, :, c], m0[i], local.at[i])
+        k.start()
+        loads.append(k)
+    at.meet()
+    v0 = remote(vec, vc, vs.at[0], vq.at[0], at.along_c)
+    v0.start()
+    c0 = []
+    for i in range(count):
+        k = remote(ins[i].at[:, :, at.co], r0[i], s0.at[i], q0.at[i], at.along_c)
+        k.start()
+        c0.append(k)
+    back = [remote(swaps[j], swap_outs[j], ws.at[j], wq.at[j], at.along_y) for j in range(2)]
+    back[0].start()
+    c1, c2, c3 = [None] * count, [None] * count, [None] * count
+
+    def add(dst, src):
+        dst[...] = (dst[...].astype(F32) + src[...].astype(F32)).astype(dst.dtype)
+
+    def first(i):
+        loads[i].wait()
+        c0[i].wait()
+        a, b = halves(ins[i].shape[-1])
+
+        def body(t, _):
+            add(m0[i].at[t // nx, t % nx], r0[i].at[t // nx, t % nx])
+            return 0
+
+        lax.fori_loop(0, nz * nx, body, 0)
+        c1[i] = (
+            remote(m0[i].at[:, :, at.yo, :, a], r1[i].at[0], s1.at[i, 0], q1.at[i, 0], at.along_y),
+            remote(m0[i].at[:, at.xo, :, :, b], r1[i].at[1], s1.at[i, 1], q1.at[i, 1], at.along_x),
+        )
+        for k in c1[i]:
+            k.start()
+
+    def second(i):
+        for k in c1[i]:
+            k.wait()
+        a, b = halves(ins[i].shape[-1])
+
+        def body(t, _):
+            u, v = t // nx, t % nx
+            add(m0[i].at[u, v, y, :, a], r1[i].at[0, u, v])
+            add(m0[i].at[u, x, v, :, b], r1[i].at[1, u, v])
+            return 0
+
+        lax.fori_loop(0, nz * nx, body, 0)
+        c2[i] = (
+            remote(m0[i].at[:, at.xo, y, :, a], r2[i].at[0], s2.at[i, 0], q2.at[i, 0], at.along_x),
+            remote(m0[i].at[:, x, at.yo, :, b], r2[i].at[1], s2.at[i, 1], q2.at[i, 1], at.along_y),
+        )
+        for k in c2[i]:
+            k.start()
+
+    def third(i):
+        for k in c2[i]:
+            k.wait()
+        a, b = halves(ins[i].shape[-1])
+
+        def body(u, _):
+            add(m0[i].at[u, x, y, :, a], r2[i].at[0, u])
+            add(m0[i].at[u, x, y, :, b], r2[i].at[1, u])
+            return 0
+
+        lax.fori_loop(0, nz, body, 0)
+        c3[i] = []
+        for d in range(1, nz):
+            k = remote(
+                m0[i].at[lax.rem(z + d, nz), x, y], r3[i].at[d - 1], s3.at[i, d - 1], q3.at[i, d - 1], at.along_z[d - 1]
+            )
+            k.start()
+            c3[i].append(k)
+
+    def fourth(i):
+        for k in c3[i]:
+            k.wait()
+        total = m0[i][z, x, y].astype(F32)
+        for d in range(1, nz):
+            total = total + r3[i][d - 1].astype(F32)
+        outs[i][...] = total
+
+    for t in range(count + 3):
+        if t < count:
+            first(t)
+        if t == 0:
+            v0.wait()
+            vm[...] = vec[...] + vc[...]
+            v1 = remote(vm, vx, vs.at[1], vq.at[1], at.along_x)
+            v1.start()
+            back[1].start()
+        if 0 <= t - 1 < count:
+            second(t - 1)
+        if t == 1:
+            v1.wait()
+            vm[...] = vm[...] + vx[...]
+            v2 = remote(vm, vy, vs.at[2], vq.at[2], at.along_y)
+            v2.start()
+        if 0 <= t - 2 < count:
+            third(t - 2)
+        if t == 2:
+            v2.wait()
+            vm[...] = vm[...] + vy[...]
+            v3 = [remote(vm, vz.at[d], vs.at[3 + d], vq.at[3 + d], at.along_z[d]) for d in range(nz - 1)]
+            for k in v3:
+                k.start()
+        if 0 <= t - 3 < count:
+            fourth(t - 3)
+    for k in v3:
+        k.wait()
+    total = vm[...]
+    for d in range(nz - 1):
+        total = total + vz[d]
+    vec_out[...] = total
+    for k in back:
+        k.wait()
+
+
+def scatter(dims, grads, vec, swaps):
+    nz, nx, nc, ny = dims
+    n = len(grads)
+    hbm, vmem = pl.BlockSpec(memory_space=pl.ANY), pl.BlockSpec(memory_space=pltpu.VMEM)
+    shapes = [g.shape[4:] for g in grads]
+    struct, sem, space = jax.ShapeDtypeStruct, pltpu.SemaphoreType.DMA, pltpu.VMEM
+    out = [struct(s, F32) for s in shapes] + [struct(vec.shape, F32)] + [struct(a.shape, a.dtype) for a in swaps]
+    scratch = (
+        [space((nz, nx, ny) + s, BF) for s in shapes] * 2
+        + [space((2, nz, nx, s[0], s[1] // 2), BF) for s in shapes]
+        + [space((2, nz, s[0], s[1] // 2), BF) for s in shapes]
+        + [space((nz - 1,) + s, BF) for s in shapes]
+        + [space(vec.shape, F32)] * 4
+        + [space((nz - 1,) + vec.shape, F32)]
+        + [sem((n,))] * 3
+        + [sem((n, 2))] * 4
+        + [sem((n, nz - 1))] * 2
+        + [sem((nz + 2,))] * 2
+        + [sem((2,))] * 2
+    )
+    return pl.pallas_call(
+        functools.partial(scatter_kernel, dims, n),
+        out_shape=out,
+        in_specs=[hbm] * n + [vmem] + [hbm] * 2,
+        out_specs=[vmem] * (n + 1) + [hbm] * 2,
+        scratch_shapes=scratch,
+        compiler_params=pltpu.CompilerParams(collective_id=1, has_side_effects=True, vmem_limit_bytes=VMEM_MOST),
+        name="scatter",
+    )(*grads, vec, *swaps)
+
+
+def lanes(shape):
+    return lax.broadcasted_iota(jnp.int32, shape, len(shape) - 1)
+
+
+def features(segments, padding):
+    lane = jnp.arange(128, dtype=jnp.int32)[None, :] % HEAD_DIM
+    same = segments[:, None] == lane
+    real = padding[:, None] == 1
+    query = jnp.where(lane < 56, same, (lane == 56) & real).astype(BF)
+    hidden = jnp.where(lane < 56, ~same, (lane == 56) & ~real)
+    key = jnp.where(hidden, neg_big, jnp.where((lane > 56) & (lane < 60), 1.0, 0.0)).astype(BF)
+    return query, key
+
+
+def pieces(value):
+    high = value.astype(BF).astype(F32)
+    value = value - high
+    middle = value.astype(BF).astype(F32)
+    return high, middle, value - middle
+
+
+def attend_kernel(tok, wq, wk, wv, bq, bv, fq, fk, q_o, k_o, v_o, mixed_o, lse_o):
+    n, d = tok.shape
+
+    def project(i, _):
+        r = pl.ds(i * BLOCK, BLOCK)
+        t = tok[r, :]
+        q_o[r, :] = (matmul(t, wq[...]) + bq[...]).astype(BF)
+        k_o[r, :] = matmul(t, wk[...]).astype(BF)
+        v_o[r, :] = (matmul(t, wv[...]) + bv[...]).astype(BF)
+        return 0
+
+    lax.fori_loop(0, n // BLOCK, project, 0)
+    lse_o[...] = jnp.zeros_like(lse_o)
+
+    def pair(p, _):
+        cols = pl.ds(pl.multiple_of(p * 128, 128), 128)
+        kp, vp, f = k_o[:, cols], v_o[:, cols], fk[...]
+        low = lanes((n, 128)) < HEAD_DIM
+        zero = jnp.zeros_like(vp)
+        ks = (jnp.where(low, kp, f), jnp.where(low, f, kp))
+        vs = (jnp.where(low, vp, zero), jnp.where(low, zero, vp))
+        lane = lanes((BLOCK, 128))
+        low = lane < HEAD_DIM
+        for b in range(n // BLOCK):
+            r = pl.ds(b * BLOCK, BLOCK)
+            qp, f = q_o[r, cols], fq[r, :]
+            qs = (jnp.where(low, qp, f), jnp.where(low, f, qp))
+            out, lse = None, lse_o[r, :]
+            for h in range(2):
+                s = transposed_right(qs[h], ks[h])
+                top = jnp.max(s, axis=1, keepdims=True)
+                e = jnp.exp2((s - top) * SCORE_SCALE)
+                total = jnp.sum(e, axis=1, keepdims=True)
+                o = matmul(e.astype(BF), vs[h]) * (1.0 / total)
+                out = o if out is None else out + o
+                lse = jnp.where(lane == 2 * p + h, top + 8.0 * jnp.log(total), lse)
+            mixed_o[r, cols] = out.astype(BF)
+            lse_o[r, :] = lse
+        return 0
+
+    lax.fori_loop(0, d // 128, pair, 0)
+
+
+def attend(tok, wq, wk, wv, bq, bv, fq, fk):
+    n, d = tok.shape
+    vmem = pl.BlockSpec(memory_space=pltpu.VMEM)
+    return pl.pallas_call(
+        attend_kernel,
+        out_shape=[jax.ShapeDtypeStruct((n, d), BF)] * 4 + [jax.ShapeDtypeStruct((n, 128), F32)],
+        in_specs=[vmem] * 8,
+        out_specs=[vmem] * 5,
+        compiler_params=pltpu.CompilerParams(vmem_limit_bytes=VMEM_MOST),
+        name="attend",
+    )(tok, wq, wk, wv, bq, bv, fq, fk)
+
+
+def attend_back_kernel(
+    tok, wq, wk, wv, q_r, k_r, v_r, mixed, do_r, lse_r, fq, fk, first_back,
+    own_o, other_o, dwq_o, dwk_o, dwv_o, dbq_o, dbv_o, dq_s, dk_s, dv_s, p_s, ds_s,
+):
+    n, d = tok.shape
+
+    def pair(p, _):
+        cols = pl.ds(pl.multiple_of(p * 128, 128), 128)
+        kp, vp, qp, op, dp = (ref[:, cols] for ref in (k_r, v_r, q_r, mixed, do_r))
+        lane = lanes((n, 128))
+        low, slot = lane < HEAD_DIM, lane % HEAD_DIM
+        fkv, fqv, lse = fk[...], fq[...].astype(F32), lse_r[...]
+        ones = jnp.where((slot > 56) & (slot < 60), 1.0, 0.0).astype(BF)
+        zero = jnp.zeros_like(vp)
+        prod = dp.astype(F32) * op.astype(F32)
+        dk = dv = dq = None
+        for h in range(2):
+            mine = low if h == 0 else jnp.logical_not(low)
+            a, b, c = pieces(-jnp.sum(jnp.where(lane == 2 * p + h, lse, 0.0), axis=1, keepdims=True))
+            f = jnp.where(slot == 57, a, jnp.where(slot == 58, b, jnp.where(slot == 59, c, fqv))).astype(BF)
+            a, b, c = pieces(-jnp.sum(jnp.where(mine, prod, 0.0), axis=1, keepdims=True))
+            g = jnp.where(slot == 57, a, jnp.where(slot == 58, b, jnp.where(slot == 59, c, 0.0))).astype(BF)
+            qx, kx = jnp.where(mine, qp, f), jnp.where(mine, kp, fkv)
+            dox, vx = jnp.where(mine, dp, g), jnp.where(mine, vp, ones)
+            q0, k0, do0 = (jnp.where(mine, v, zero) for v in (qp, kp, dp))
+            for kb in range(n // BLOCK):
+                r = slice(kb * BLOCK, (kb + 1) * BLOCK)
+                e = jnp.exp2(transposed_right(kx[r], qx) * SCORE_SCALE)
+                t = transposed_right(vx[r], dox)
+                p_s[r, :] = e.astype(BF)
+                ds_s[r, :] = (e * t).astype(BF)
+            parts = (matmul(p_s[...], do0), matmul(ds_s[...], q0), transposed_left(ds_s[...], k0))
+            dv, dk, dq = parts if dv is None else (dv + parts[0], dk + parts[1], dq + parts[2])
+        dq_s[:, cols] = (dq * 0.125).astype(BF)
+        dk_s[:, cols] = (dk * 0.125).astype(BF)
+        dv_s[:, cols] = dv.astype(BF)
+        return 0
+
+    lax.fori_loop(0, d // 128, pair, 0)
+    dbq_o[...] = jnp.sum(dq_s[...].astype(F32), axis=0, keepdims=True)
+    dbv_o[...] = jnp.sum(dv_s[...].astype(F32), axis=0, keepdims=True)
+    t = tok[...]
+    dwq_o[...] = transposed_left(t, dq_s[...]).astype(BF)
+    dwk_o[...] = transposed_left(t, dk_s[...]).astype(BF)
+    dwv_o[...] = transposed_left(t, dv_s[...]).astype(BF)
+
+    def tail(i, shift, out):
+        r, w = pl.ds(shift + i * BLOCK, BLOCK), pl.ds(i * BLOCK, BLOCK)
+        total = (
+            transposed_right(dq_s[r, :], wq[...])
+            + transposed_right(dk_s[r, :], wk[...])
+            + transposed_right(dv_s[r, :], wv[...])
+            + first_back[r, :]
+        )
+        out[w, :] = total.astype(out.dtype)
+        return 0
+
+    lax.fori_loop(0, n // 2 // BLOCK, lambda i, _: tail(i, 0, own_o), 0)
+    lax.fori_loop(0, n // 2 // BLOCK, lambda i, _: tail(i, n // 2, other_o), 0)
+
+
+def attend_back(tok, wq, wk, wv, q, k, v, mixed, do, lse, fq, fk, first_back):
+    n, d = tok.shape
+    vmem, struct = pl.BlockSpec(memory_space=pltpu.VMEM), jax.ShapeDtypeStruct
+    return pl.pallas_call(
+        attend_back_kernel,
+        out_shape=[struct((n // 2, d), F32), struct((n // 2, d), BF)]
+        + [struct((d, d), BF)] * 3
+        + [struct((1, d), F32)] * 2,
+        in_specs=[vmem] * 13,
+        out_specs=[vmem] * 7,
+        scratch_shapes=[pltpu.VMEM((n, d), BF)] * 3 + [pltpu.VMEM((n, n), BF)] * 2,
+        compiler_params=pltpu.CompilerParams(vmem_limit_bytes=VMEM_MOST),
+        name="attend_back",
+    )(tok, wq, wk, wv, q, k, v, mixed, do, lse, fq, fk, first_back)
+
+
+def row_mean(value):
+    return jnp.mean(value, axis=1, keepdims=True)
+
+
+def column_sum(value):
+    return jnp.sum(value, axis=0, keepdims=True)
+
+
+def middle_kernel(
+    place, tok, low, mixed, cot, cot_low, wp, wi, wo, bp, g1, s1, bi, bo, g2, s2,
+    own_o, other_o, first_o, back_o, dwo_o, dwi_o, dwp_o, vec_o, dbi_o,
+    act_s, ib_s, slope_s, hl_s, ol_s, br_s, mx_s, *, steps,
+):
+    i = pl.program_id(0)
+    wide, part = wi.shape[1], dwo_o.shape[0]
+
+    @pl.when(i < steps)
+    def _():
+        r = pl.ds(pl.multiple_of(i * BLOCK, BLOCK), BLOCK)
+
+        @pl.when(i == 0)
+        def _():
+            vec_o[...] = jnp.zeros_like(vec_o)
+            dbi_o[...] = jnp.zeros_like(dbi_o)
+
+        is_own = i < steps // 2
+        mx = mixed[...]
+        mx_s[r, :] = mx
+        first_sum = jnp.where(is_own, tok[0], low[0].astype(F32)) + matmul(mx, wp[...]) + bp[...]
+        center = first_sum - row_mean(first_sum)
+        scale1 = lax.rsqrt(row_mean(center * center) + 1e-05)
+        n1 = center * scale1
+        hidden = n1 * g1[...] + s1[...]
+        hl = hidden.astype(BF)
+        hl_s[r, :] = hl
+        for j in range(wide // part):
+            c = slice(j * part, (j + 1) * part)
+            v = matmul(hl, wi[:, c]) + bi[:, c]
+            phi = 0.5 + 0.5 * lax.erf(v * 0.7071067811865476)
+            act_s[r, c] = (v * phi).astype(BF)
+            slope_s[:, c] = phi + v * (jnp.exp2(v * v * (-0.5 * LOG2E)) * 0.3989422804014327)
+        second_sum = hidden + matmul(act_s[r, :], wo[...]) + bo[...]
+        center = second_sum - row_mean(second_sum)
+        scale2 = lax.rsqrt(row_mean(center * center) + 1e-05)
+        n2 = center * scale2
+        result = n2 * g2[...] + s2[...]
+
+        @pl.when(is_own)
+        def _():
+            own_o[...] = result
+
+        @pl.when(jnp.logical_not(is_own))
+        def _():
+            other_o[...] = result.astype(BF)
+
+        ct = jnp.where(is_own, cot[0], cot_low[...].astype(F32))
+        cg = ct * g2[...]
+        second_back = (cg - row_mean(cg) - n2 * row_mean(cg * n2)) * scale2
+        ol = second_back.astype(BF)
+        ol_s[r, :] = ol
+        for j in range(wide // part):
+            c = slice(j * part, (j + 1) * part)
+            ib = (transposed_right(ol, wo[c, :]) * slope_s[:, c]).astype(BF)
+            ib_s[r, c] = ib
+            dbi_o[:, c] += column_sum(ib.astype(F32))
+        hidden_back = transposed_right(ib_s[r, :], wi[...]) + second_back
+        cg = hidden_back * g1[...]
+        first_back = (cg - row_mean(cg) - n1 * row_mean(cg * n1)) * scale1
+        first_o[...] = first_back
+        br = first_back.astype(BF)
+        br_s[r, :] = br
+        back_o[...] = transposed_right(br, wp[...]).astype(BF)
+        sums = (ct * n2, ct, ol.astype(F32), hidden_back * n1, hidden_back, br.astype(F32))
+        for k, value in enumerate(sums):
+            vec_o[k : k + 1, :] += column_sum(value)
+
+    @pl.when(i >= steps)
+    def _():
+        j = i - steps
+        c = pl.ds(pl.multiple_of(j * part, part), part)
+        dwo_o[...] = transposed_left(act_s[:, c], ol_s[...]).astype(BF)
+        dwi_o[...] = transposed_left(hl_s[...], ib_s[:, c]).astype(BF)
+
+        @pl.when(j == 0)
+        def _():
+            dwp_o[...] = transposed_left(mx_s[...], br_s[...]).astype(BF)
+
+
+def middle(place, tok, low, mixed, cot, cot_low, wp, wi, wo, bp, g1, s1, bi, bo, g2, s2):
+    n, d = mixed.shape
+    ff = wi.shape[1]
+    steps, part = n // BLOCK, min(ff, 768)
+    half, more = steps // 2, ff // part
+    struct, clip = jax.ShapeDtypeStruct, jnp.clip
+    own = lambda i, y: (y[0], clip(i, 0, half - 1), 0)
+    row = lambda i, y: (clip(i, 0, steps - 1), 0)
+    first, last = (lambda i, y: (clip(i, 0, half - 1), 0)), (lambda i, y: (clip(i - half, 0, half - 1), 0))
+    tile = lambda i: jnp.maximum(i - steps, 0)
+    full = lambda a: pl.BlockSpec(a.shape, lambda i, y: (0,) * a.ndim, pipeline_mode=pl.Buffered(1))
+    block = lambda index: pl.BlockSpec((BLOCK, d), index)
+    still = lambda i, y: (0, 0)
+    vecs = [bp, g1, s1, bi, bo, g2, s2]
+    return pl.pallas_call(
+        functools.partial(middle_kernel, steps=steps),
+        grid_spec=pltpu.PrefetchScalarGridSpec(
+            num_scalar_prefetch=1,
+            grid=(steps + more,),
+            in_specs=[
+                pl.BlockSpec((1, BLOCK, d), own),
+                pl.BlockSpec((1, BLOCK, d), lambda i, y: (1, clip(i - half, 0, half - 1), 0)),
+                block(row),
+                pl.BlockSpec((1, BLOCK, d), own),
+                block(last),
+            ]
+            + [full(w) for w in (wp, wi, wo)]
+            + [full(v) for v in vecs],
+            out_specs=[
+                block(first),
+                block(last),
+                block(row),
+                block(row),
+                pl.BlockSpec((part, d), lambda i, y: (tile(i), 0)),
+                pl.BlockSpec((d, part), lambda i, y: (0, tile(i))),
+                pl.BlockSpec((d, d), still),
+                pl.BlockSpec((8, d), still),
+                pl.BlockSpec((1, ff), still),
+            ],
+            scratch_shapes=[pltpu.VMEM((n, ff), BF)] * 2
+            + [pltpu.VMEM((BLOCK, ff), F32)]
+            + [pltpu.VMEM((n, d), BF)] * 4,
+        ),
+        out_shape=[struct((n // 2, d), F32), struct((n // 2, d), BF), struct((n, d), F32), struct((n, d), BF)]
+        + [struct((ff, d), BF), struct((d, ff), BF), struct((d, d), BF), struct((8, d), F32), struct((1, ff), F32)],
+        compiler_params=pltpu.CompilerParams(vmem_limit_bytes=VMEM_MOST, dimension_semantics=("arbitrary",)),
+        name="middle",
+    )(place, tok, low, mixed, cot, cot_low, wp, wi, wo, *vecs)
+
+
+def swapped_layer(
+    mesh, tokens, segments, padding, query_weight, query_bias, key_weight, value_weight, value_bias,
+    output_weight, output_bias, first_gain, first_shift, inner_weight, inner_bias, outer_weight,
+    outer_bias, second_gain, second_shift, cotangent,
+):
+    dims = grid_dims(mesh)
+    parts = dims[0] * dims[1] * dims[2] * dims[3]
+    y = lax.axis_index("seq")
+    mine = lax.axis_index("dp") * 2 + y
+    count, rows, d = tokens.shape
+    small = [query_bias, value_bias, output_bias, first_gain, first_shift, outer_bias, second_gain, second_shift]
+    width = d // parts
+    strip = jnp.concatenate(small + [inner_bias]).astype(F32)
+    size = -(-strip.shape[0] // 128) * 128
+    strip = jnp.broadcast_to(jnp.pad(strip, (0, size - strip.shape[0]))[None], (8, size))
+    weights = [query_weight, key_weight, value_weight, output_weight, inner_weight, outer_weight]
+    got = gather(dims, [strip] + weights, tokens, cotangent)
+    table = got[0].reshape(parts, 8, size)[:, 0]
+    wq, wk, wv, wp, wi, wo = (g.reshape(-1, g.shape[-1]) for g in got[1:7])
+    low, cot_low = got[7], got[8]
+    vectors = table[:, : 8 * width].reshape(parts, 8, width).transpose(1, 0, 2).reshape(8, d)
+    bq, bv, bp, g1, s1, bo, g2, s2 = (vectors[k : k + 1] for k in range(8))
+    bi = table[:, 8 * width : 8 * width + inner_bias.shape[0]].reshape(1, -1)
+
+    def in_order(array):
+        line = lax.dynamic_index_in_dim(array, y, 0, keepdims=False).reshape(2, rows)
+        return jnp.where(y == 0, line, line[::-1]).reshape(-1)
+
+    fq, fk = features(in_order(segments), in_order(padding))
+    tok = low.reshape(2 * rows, d)
+    q, k, v, mixed, lse = attend(tok, wq, wk, wv, bq, bv, fq, fk)
+    out_own, out_other, first_back, do, dwo, dwi, dwp, vec, dbi = middle(
+        y.reshape(1), tokens, low, mixed, cotangent, cot_low, wp, wi, wo, bp, g1, s1, bi, bo, g2, s2
+    )
+    in_own, in_other, dwq, dwk, dwv, dbq, dbv = attend_back(
+        tok, wq, wk, wv, q, k, v, mixed, do, lse, fq, fk, first_back
+    )
+    sums = jnp.concatenate([vec[:6], dbq, dbv, dbi.reshape(-1, d)])
+    sums = jnp.pad(sums, ((0, -sums.shape[0] % 8), (0, 0)))
+    grads = [g.reshape(dims + (g.shape[0] // parts, g.shape[1])) for g in (dwo, dwi, dwp, dwq, dwk, dwv)]
+    dwo, dwi, dwp, dwq, dwk, dwv, sums, out_got, in_got = scatter(dims, grads, sums, [out_other, in_other])
+    own = lax.dynamic_slice(sums, (0, mine * width), (8, width))
+    dg2, ds2, dbo, dg1, ds1, dbp, dbq, dbv = (own[k] for k in range(8))
+    inner_width = inner_bias.shape[0]
+    dbi = lax.dynamic_slice(sums[8 : 8 + inner_width * parts // d].reshape(-1), (mine * inner_width,), (inner_width,))
+
+    def whole(own, got):
+        got = got.astype(F32)
+        return jnp.where(y == 0, jnp.stack([own, got]), jnp.stack([got, own]))
+
+    return (
+        whole(out_own, out_got), whole(in_own, in_got), dwq, dbq, dwk, dwv, dbv, dwp, dbp, dg1, ds1,
+        dwi, dbi, dwo, dbo, dg2, ds2,
+    )
+
+
 def solution(mesh):
     placed = (
         P("dp", "seq", None),
@@ -341,8 +1030,13 @@
         P(("dp", "seq")),
         P("dp", "seq", None),
     )
+    def layer(*args):
+        if swappable(mesh, args[0].shape):
+            return swapped_layer(mesh, *args)
+        return gathered_layer(*args)
+
     return jax.shard_map(
-        per_device,
+        layer,
         mesh=mesh,
         in_specs=placed,
         out_specs=(

time: 1480 us -> 413 us (0.28)
  waiting for transfers between devices: 937 us -> 0 us
  Pallas kernels: 0 us -> 371 us
  matrix products: 332 us -> 0 us
  blocking collectives: 82.7 us -> 0 us
  local copies, waits for them, and re-layouts: 63.7 us -> 30.4 us
  other arithmetic: 40.8 us -> 10.1 us
    pallas_call x0 -> x5, Pallas kernels: none -> 371 us  [the longest x1 119 us: scatter(): pl.pallas_call(functools.partial(scatter_kernel, dims, n), out_shape=out,...]
    reduce_scatter x5 -> x0, waiting for transfers between devices: 356 us -> none  [the longest x1 142 us: per_device(): lax.psum_scatter(inner_delta, ('dp', 'seq'), scatter_dimension=0, tiled=T...]
    dot_general x102 -> x0, matrix products: 332 us -> none  [the longest x24 68 us: head_slices(): jnp.einsum('sqd,skd->sqk', query_head, key_head, preferred_element_type=j...]
    unnamed x19 -> x0, waiting for transfers between devices: 317 us -> none
    all_gather x8 -> x0, waiting for transfers between devices: 264 us -> none  [the longest x1 51.4 us: per_device(): lax.all_gather(key_weight, ('dp', 'seq'), axis=0, tiled=True)]
    unnamed x2 -> x0, blocking collectives: 82.7 us -> none
    unnamed x82 -> x28, local copies, waits for them, and re-layouts: 33.2 us -> 6.17 us
    reduce_sum x22 -> x0, other arithmetic: 25 us -> none  [the longest x12 13.3 us: forward_head(): row_total = jnp.sum(exponent, axis=2, keepdims=True)]
  transfers between devices with their start and end apart: 16 -> 0, of which waited for: 15 -> 0; matrix products, arithmetic and copies ran while one was open for 15% -> 0% of each run, Pallas kernels for 0% -> 0%
where the time goes in v1:
time: 413 us; the launch traced here: 412 us
  Pallas kernels  371 us (90%)
  local copies, waits for them, and re-layouts  30.4 us (7%)
  other arithmetic  10.1 us (2%)
    pallas_call x1, Pallas kernels, scatter(): pl.pallas_call(functools.partial(scatter_kernel, dims, n), out_shape=out,...  119 us
    pallas_call x1, Pallas kernels, gather(): pl.pallas_call(functools.partial(gather_kernel, dims, n), out_shape=out,...  106 us
    pallas_call x1, Pallas kernels, attend_back(): pl.pallas_call(attend_back_kernel, out_shape=[struct((n // 2, d), F32), s...  56.5 us
    pallas_call x1, Pallas kernels, middle(): pl.pallas_call(functools.partial(middle_kernel, steps=steps), grid_spec=p...  55.8 us
    pallas_call x1, Pallas kernels, attend(): pl.pallas_call(attend_kernel, out_shape=[jax.ShapeDtypeStruct((n, d), BF)...  33.4 us
    slice x9, local copies, waits for them, and re-layouts, swapped_layer(): bq, bv, bp, g1, s1, bo, g2, s2 = (vectors[k:k + 1] for k in range(8))  10.6 us

profile of v1, /device:TPU:0, one launch (start us, length us, event | category | flops | bytes accessed | tf_op | source)
XLA Modules:
  0.0 412.3 jit_solution(6331359188934659987)
XLA Ops:
  1.8 1.0 select_convert_fusion.fk
  2.9 1.0 fusion.fq
  3.9 6.1 %concatenate.6 = bf16[288]{0:T(512)(128)(2,1)S(1)} concatenate(bf16[24]{0:T(256)(128)(2,1)} %param.23, bf16[24]{0:T(256)(128)(2,1)} %param.26, bf16[24]{0:T(256)(128)(2,1)} %param.28, bf16[24]{0:T(256)(128)(2,1)} %param.29, bf16[24]{0:T(256)(128)(2,1)} %param.30, bf16[24]{0:T(256)(128)(2,1)} %param.34, bf16[24]{0:T(256)(128)(2,1)} %param.35, bf16[24]{0:T(256)(128)(2,1)} %param.36, ...), dimensions={0} | concatenate | bytes 1152 | tf_op jit(solution)/shard_map/concatenate | solution.py:967
  10.6 105.9 %gather.1 = (f32[4,2,2,2,8,384]{5,4,3,2,1,0:T(8,128)}, bf16[4,2,2,2,24,768]{5,4,3,2,1,0:T(8,128)(2,1)}, bf16[4,2,2,2,24,768]{5,4,3,2,1,0:T(8,128)(2,1)}, bf16[4,...) custom-call(f32[8,384]{1,0:T(8,128)} %broadcast_in_dim.40.refs_0_, ...), custom_call_target="tpu_custom_call" | custom-call | tf_op jit(solution)/shard_map/gather/pallas_call | solution.py:485
  116.5 1.0 slice.116
  118.3 0.9 slice_reduce_fusion
  120.6 33.4 %attend.1 = (bf16[1024,768]{1,0:T(8,128)(2,1)}, bf16[1024,768]{1,0:T(8,128)(2,1)}, bf16[1024,768]{1,0:T(8,128)(2,1)}, bf16[1024,768]{1,0:T(8,128)(2,1)}, f32[1024,128]{1,0:T(8,128)}) custom-call(bf16[1024,768]{1,0:T(8,128)(2,1)} %bitcast.47, bf16[768,768]{1,0:T(8,128)(2,1)} %bitcast.51, bf16[768,768]{1,0:T(8,128)(2,1)} %bitcast.53, ...), custom_call_target="tpu_custom_call" | custom-call | tf_op jit(solution)/shard_map/attend/pallas_call | solution.py:730
  154.0 1.4 slice.101.bo
  155.4 1.4 slice.103.g2
  156.8 1.4 slice.105.s2
  158.2 1.4 slice.94.bp
  159.6 1.4 slice.96.g1
  161.0 1.4 slice.98.s1
  162.4 0.8 slice.123
  163.9 55.8 %middle.1 = (f32[512,768]{1,0:T(8,128)}, bf16[512,768]{1,0:T(8,128)(2,1)}, f32[1024,768]{1,0:T(8,128)}, bf16[1024,768]{1,0:T(8,128)(2,1)}, bf16[3072,768]{1,0:T(...) custom-call(s32[1]{0:T(128)} %bitcast.place, ...), custom_call_target="tpu_custom_call" | custom-call | tf_op jit(solution)/shard_map/middle/pallas_call | solution.py:919
  219.7 56.5 %attend_back.1 = (f32[512,768]{1,0:T(8,128)}, bf16[512,768]{1,0:T(8,128)(2,1)}, bf16[768,768]{1,0:T(8,128)(2,1)}, bf16[768,768]{1,0:T(8,128)(2,1)}, bf16[768,768...) custom-call(bf16[1024,768]{1,0:T(8,128)(2,1)} %bitcast.48, bf16[768,768]{1,0:T(8,128)(2,1)} %bitcast.52, ...), custom_call_target="tpu_custom_call" | custom-call | tf_op jit(solution)/shard_map/attend_back/pallas_call | solution.py:804
  276.7 1.4 reduce.43
  278.1 1.4 select_maximum_fusion.refs_6_
  279.5 119.4 %scatter.1 = (f32[96,768]{1,0:T(8,128)}, f32[24,3072]{1,0:T(8,128)}, f32[24,768]{1,0:T(8,128)}, f32[24,768]{1,0:T(8,128)}, f32[24,768]{1,0:T(8,128)}, /*index=5*...) custom-call(bf16[4,2,2,2,96,768]{5,4,3,2,1,0:T(8,128)(2,1)} %bitcast.49, ...), custom_call_target="tpu_custom_call" | custom-call | tf_op jit(solution)/shard_map/scatter/pallas_call | solution.py:652
  398.9 1.4 bitcast_convert_fusion
  400.5 1.9 maximum_select_fusion.1
  402.5 1.3 copy-done
  403.8 1.9 maximum_select_fusion
  407.0 0.8 constant_dynamic-slice_fusion
  (53 shorter events, 11.2 us)
Async XLA Ops:
  117.6 0.6 copy-start.5
  398.8 1.6 copy-start.1
  400.5 1.9 copy-start.2
  402.4 1.4 copy-start
  403.8 4.6 %copy-start.9 = (f32[24,768]{1,0:T(8,128)S(1)}, f32[24,768]{1,0:T(8,128)}, u32[]{:S(2)}) copy-start(f32[24,768]{1,0:T(8,128)} %get-tuple-element.134) | copy-start | bytes 221188
  403.8 5.2 %copy-start.8 = (f32[24,768]{1,0:T(8,128)S(1)}, f32[24,768]{1,0:T(8,128)}, u32[]{:S(2)}) copy-start(f32[24,768]{1,0:T(8,128)} %get-tuple-element.136) | copy-start | bytes 221188
  403.8 5.8 %copy-start.7 = (f32[24,768]{1,0:T(8,128)S(1)}, f32[24,768]{1,0:T(8,128)}, u32[]{:S(2)}) copy-start(f32[24,768]{1,0:T(8,128)} %get-tuple-element.137) | copy-start | bytes 221188
  403.8 6.5 %copy-start.6 = (f32[24,768]{1,0:T(8,128)S(1)}, f32[24,768]{1,0:T(8,128)}, u32[]{:S(2)}) copy-start(f32[24,768]{1,0:T(8,128)} %get-tuple-element.139) | copy-start | bytes 221188
  403.8 7.1 %copy-start.4 = (f32[24,3072]{1,0:T(8,128)S(1)}, f32[24,3072]{1,0:T(8,128)}, u32[]{:S(2)}) copy-start(f32[24,3072]{1,0:T(8,128)} %get-tuple-element.143) | copy-start | bytes 884740
  403.8 7.8 %copy-start.3 = (f32[96,768]{1,0:T(8,128)S(1)}, f32[96,768]{1,0:T(8,128)}, u32[]{:S(2)}) copy-start(f32[96,768]{1,0:T(8,128)} %get-tuple-element.145) | copy-start | bytes 884740
